TPU v7x, 512 devices: a whole 4x8x8 slice. The times are simulated.
512 devices in a mesh: rows: 64 (over x, z, core), cols: 8 (over y).
Axes of the slice: x: 4, y: 8, z: 8, core: 2. Of those that a mesh axis runs over, the one named last changes fastest.
Arguments:
- right_sides: float32 [4, 64, 128, 256], P(None, 'rows'), may hold values from -6 to 6
- factor_blocks: bfloat16 [3, 64, 8, 8, 256, 256], P(None, 'rows', 'cols'), may hold values from -0.125 to 0.125
- diag_inverses: bfloat16 [4, 64, 256, 256], P(None, 'rows')
- source_ids: int32 [3, 64, 8, 8], P(None, 'rows', 'cols'), may hold values from 0 to 191, as said below
- block_counts: int32 [3, 64, 8], P(None, 'rows', 'cols'), may hold values from 1 to 8, as said below
Outputs:
- solution: float32 [4, 64, 128, 256], P(None, 'rows', 'cols')
Inputs may be any that keep to these rules, and one draw needn't show every extreme that they name: source_ids[l, t, c, k] = m * 64 + s names a supernode of a level m <= l with s % 8 == c. block_counts[l, t, c] slots of target t on group c hold blocks of the factor; slots at and past it are not part of the factor. In every level some target and group has all 8 slots live.
All inputs are finite; a program needn't handle non-finite values.
Results may differ from a plain program's by a relative error of at most 0.007.
Values may be sent and summed in bfloat16 or wider, within the bound.
A program may use at most 128 MiB of HBM per device.

v0:
```python
import jax
import jax.numpy as jnp
from jax import lax
from jax.sharding import PartitionSpec as P


def locate(source, row_count, col_count):
    return source // row_count * (row_count // col_count) + source % row_count // col_count


def slot_sum(running, blocks, chosen_ids, live_count, solved_store, row_count, col_count):

    def add_block(slot_index, partial_value):
        source = chosen_ids[slot_index]
        solved_piece = lax.dynamic_index_in_dim(
            solved_store, locate(source, row_count, col_count), 0, keepdims=False
        )
        factor_piece = lax.dynamic_index_in_dim(blocks, slot_index, 0, keepdims=False)
        return partial_value + jnp.dot(
            solved_piece, factor_piece, preferred_element_type=jnp.float32
        )

    return lax.fori_loop(0, live_count, add_block, running)


def shards(right_sides, factor_blocks, diag_inverses, source_ids, block_counts):
    row_count = lax.axis_size("rows")
    col_count = lax.axis_size("cols")
    level_count = right_sides.shape[0]
    rhs_count = right_sides.shape[2]
    block_width = right_sides.shape[3]
    share_rows = rhs_count // col_count
    col_index = lax.axis_index("cols")
    per_level = row_count // col_count
    solved_store = jnp.zeros(((level_count - 1) * per_level, rhs_count, block_width), jnp.bfloat16)
    partials = [jnp.zeros((rhs_count, block_width), jnp.float32)] * level_count
    solutions = []
    for level_index in range(level_count):
        if level_index > 0:
            partials[level_index] = slot_sum(
                partials[level_index],
                factor_blocks[level_index - 1, 0, 0],
                source_ids[level_index - 1, 0, 0],
                block_counts[level_index - 1, 0, 0],
                solved_store,
                row_count,
                col_count,
            )
        own_rhs = lax.dynamic_slice_in_dim(
            right_sides[level_index, 0], col_index * share_rows, share_rows, 0
        )
        if level_index > 0:
            own_rhs = own_rhs - lax.psum_scatter(
                partials[level_index], "cols", scatter_dimension=0, tiled=True
            )
        own_solution = jnp.dot(
            own_rhs.astype(jnp.bfloat16),
            diag_inverses[level_index, 0],
            preferred_element_type=jnp.float32,
        )
        solutions.append(own_solution)
        if level_index < level_count - 1:
            pieces = lax.all_gather(
                own_solution.astype(jnp.bfloat16)[None], "rows", axis=0, tiled=True
            )
            grouped = pieces.reshape(per_level, col_count, share_rows, block_width)
            regrouped = lax.all_to_all(grouped, "cols", split_axis=1, concat_axis=2, tiled=True)
            solved_store = solved_store.at[
                level_index * per_level : (level_index + 1) * per_level
            ].set(regrouped[:, 0])
    return jnp.stack(solutions)[:, None]


def solution(mesh):
    return jax.shard_map(
        shards,
        mesh=mesh,
        in_specs=(
            P(None, "rows", None, None),
            P(None, "rows", "cols", None, None, None),
            P(None, "rows", None, None),
            P(None, "rows", "cols", None),
            P(None, "rows", "cols"),
        ),
        out_specs=P(None, "rows", "cols", None),
        check_vma=False,
    )
```

profile of v0, /device:TPU:2, one launch (start us, length us, event | category | flops | bytes accessed | tf_op | source)
XLA Modules:
  0.0 462.0 jit_solution(18360709935676070336)
XLA Ops:
  6.5 0.9 slice.116
  7.5 1.0 fusion.40
  8.5 56.0 %all-gather = bf16[1024,256]{1,0:T(8,128)(2,1)S(1)} all-gather(bf16[16,256]{1,0:T(8,128)(2,1)S(1)} %get-tuple-element.425), channel_id=2, replica_groups=mesh['rows'=64,'cols'=8] {'rows'}, dimensions={0}, use_global_device_ids=true | all-gather | bytes 532480 | tf_op jit(solution)/shard_map/all_gather | solution.py:63
  64.5 0.8 copy.11
  65.4 7.1 %all-to-all-start = ((bf16[8,8,16,256]{3,2,0,1:T(8,128)(2,1)}), bf16[8,8,16,256]{3,2,0,1:T(8,128)(2,1)S(1)}, u32[]{:S(2)}, u32[]{:S(2)}) async-start(bf16[8,8,16,256]{3,2,0,1:T(8,128)(2,1)} %copy.11), calls=%async_computation | async-start | bytes 1048576 | tf_op jit(solution)/shard_map/all_to_all | solution.py:67
  72.5 0.0 reduce-scatter.4.cloned.1.call-start
  72.5 0.0 copy-done.4
  72.5 0.6 fusion.39
  73.1 0.0 copy-done.5
  73.1 0.6 slice_bitcast_fusion.4
  73.7 3.5 slice_bitcast_fusion
  77.2 13.3 %all-to-all-done = bf16[8,8,16,256]{3,2,0,1:T(8,128)(2,1)S(1)} async-done(((bf16[8,8,16,256]{3,2,0,1:T(8,128)(2,1)}), bf16[8,8,16,256]{3,2,0,1:T(8,128)(2,1)S(1)}, u32[]{:S(2)}, u32[]{:S(2)}) %all-to-all-start) | async-done | bytes 524320 | tf_op jit(solution)/shard_map/all_to_all | solution.py:67
  90.5 0.1 scatter.10
  90.7 0.0 copy-start.3
  90.7 21.3 %while.42 = (s32[]{:T(128)}, f32[128,256]{1,0:T(8,128)S(1)}, s32[]{:T(128)}, s32[8]{0:T(128)S(1)}, bf16[24,128,256]{2,1,0:T(8,128)(2,1)S(1)}, /*index=5*/bf16[8,...) while((s32[]{:T(128)}, f32[128,256]{1,0:T(8,128)S(1)}, ...), condition=%wide.region_1.2_spmd, body=%wide.region_0.0_spmd.sunk | while | flops 16810028 | bytes 459350 | solution.py:23
  91.4 0.7 dynamic_slice.141
  94.8 1.1 convolution_add_fusion.6
  96.5 0.7 dynamic_slice.141
  100.0 1.1 convolution_add_fusion.6
  101.7 0.7 dynamic_slice.141
  105.2 1.1 convolution_add_fusion.6
  106.8 0.7 dynamic_slice.141
  110.3 1.1 convolution_add_fusion.6
  112.0 0.0 copy-start.1
  112.0 0.7 copy-done.1
  112.6 0.0 reduce-scatter.4.cloned.1.call-update
  112.7 0.0 copy-done.3
  112.7 51.3 %reduce-scatter.4.cloned.1.call-done = f32[16,256]{1,0:T(8,128)} async-done(((f32[128,256]{1,0:T(8,128)}), f32[16,256]{1,0:T(8,128)}) %reduce-scatter.4.cloned.1.call-update) | async-done | bytes 16400 | tf_op jit(solution)/shard_map/reduce_scatter | solution.py:53
  164.0 1.1 fusion.41
  165.0 50.9 %all-gather.1 = bf16[1024,256]{1,0:T(8,128)(2,1)S(1)} all-gather(bf16[16,256]{1,0:T(8,128)(2,1)S(1)} %get-tuple-element.427), channel_id=3, replica_groups=mesh['rows'=64,'cols'=8] {'rows'}, dimensions={0}, use_global_device_ids=true | all-gather | bytes 532480 | tf_op jit(solution)/shard_map/all_gather | solution.py:63
  215.9 0.8 copy.13
  216.7 4.6 all-to-all-start.1
  221.3 0.0 reduce-scatter.6.cloned.1.call-start
  221.4 18.0 %all-to-all-done.1 = bf16[8,8,16,256]{3,2,0,1:T(8,128)(2,1)S(1)} async-done(((bf16[8,8,16,256]{3,2,0,1:T(8,128)(2,1)}), bf16[8,8,16,256]{3,2,0,1:T(8,128)(2,1)S(1)}, u32[]{:S(2)}, u32[]{:S(2)}) %all-to-all-start.1) | async-done | bytes 524320 | tf_op jit(solution)/shard_map/all_to_all | solution.py:67
  239.4 0.0 copy-done.7
  239.4 15.6 %while.43 = (s32[]{:T(128)}, f32[128,256]{1,0:T(8,128)S(1)}, s32[]{:T(128)}, s32[8]{0:T(128)S(1)}, bf16[24,128,256]{2,1,0:T(8,128)(2,1)S(1)}, /*index=5*/bf16[8,...) while((s32[]{:T(128)}, f32[128,256]{1,0:T(8,128)S(1)}, ...), condition=%wide.region_4.5_spmd, body=%wide.region_3.4_spmd.sunk | while | flops 16810028 | bytes 459350 | solution.py:23
  240.1 0.7 dynamic_slice.144
  243.3 1.1 convolution_add_fusion.7
  245.1 0.7 dynamic_slice.144
  248.3 1.1 convolution_add_fusion.7
  250.1 0.7 dynamic_slice.144
  253.3 1.1 convolution_add_fusion.7
  255.1 0.0 copy-start.2
  255.1 0.6 copy-done.2
  255.7 0.0 reduce-scatter.6.cloned.1.call-update
  255.7 57.3 %reduce-scatter.6.cloned.1.call-done = f32[16,256]{1,0:T(8,128)} async-done(((f32[128,256]{1,0:T(8,128)}), f32[16,256]{1,0:T(8,128)}) %reduce-scatter.6.cloned.1.call-update) | async-done | bytes 16400 | tf_op jit(solution)/shard_map/reduce_scatter | solution.py:53
  313.1 1.1 fusion.42
  314.1 50.8 %all-gather.2 = bf16[1024,256]{1,0:T(8,128)(2,1)S(1)} all-gather(bf16[16,256]{1,0:T(8,128)(2,1)S(1)} %get-tuple-element.429), channel_id=4, replica_groups=mesh['rows'=64,'cols'=8] {'rows'}, dimensions={0}, use_global_device_ids=true | all-gather | bytes 532480 | tf_op jit(solution)/shard_map/all_gather | solution.py:63
  364.9 0.9 copy.15
  365.8 4.6 %all-to-all-start.2 = ((bf16[8,8,16,256]{3,2,0,1:T(8,128)(2,1)}), bf16[8,8,16,256]{3,2,0,1:T(8,128)(2,1)S(1)}, u32[]{:S(2)}, u32[]{:S(2)}) async-start(bf16[8,8,16,256]{3,2,0,1:T(8,128)(2,1)} %copy.15), calls=%async_computation.4 | async-start | bytes 1048576 | tf_op jit(solution)/shard_map/all_to_all | solution.py:67
  370.4 0.0 reduce-scatter.8.cloned.1.call-start
  370.5 18.0 %all-to-all-done.2 = bf16[8,8,16,256]{3,2,0,1:T(8,128)(2,1)S(1)} async-done(((bf16[8,8,16,256]{3,2,0,1:T(8,128)(2,1)}), bf16[8,8,16,256]{3,2,0,1:T(8,128)(2,1)S(1)}, u32[]{:S(2)}, u32[]{:S(2)}) %all-to-all-start.2) | async-done | bytes 524320 | tf_op jit(solution)/shard_map/all_to_all | solution.py:67
  388.6 12.5 %while.44 = (s32[]{:T(128)}, f32[128,256]{1,0:T(8,128)S(1)}, s32[]{:T(128)}, s32[8]{0:T(128)S(1)}, bf16[24,128,256]{2,1,0:T(8,128)(2,1)S(1)}, /*index=5*/bf16[8,...) while((s32[]{:T(128)}, f32[128,256]{1,0:T(8,128)S(1)}, ...), condition=%wide.region_7.8_spmd, body=%wide.region_6.7_spmd.sunk | while | flops 16810028 | bytes 459350 | solution.py:23
  389.2 0.6 dynamic_slice.147
  392.4 0.2 convolution_add_fusion.8
  393.2 0.6 dynamic_slice.147
  396.3 0.2 convolution_add_fusion.8
  397.2 0.6 dynamic_slice.147
  400.3 0.2 convolution_add_fusion.8
  401.1 0.6 copy-done
  401.8 0.0 reduce-scatter.8.cloned.1.call-update
  401.8 51.9 %reduce-scatter.8.cloned.1.call-done = f32[16,256]{1,0:T(8,128)} async-done(((f32[128,256]{1,0:T(8,128)}), f32[16,256]{1,0:T(8,128)}) %reduce-scatter.8.cloned.1.call-update) | async-done | bytes 16400 | tf_op jit(solution)/shard_map/reduce_scatter | solution.py:53
  453.7 1.1 convolution_bitcast_fusion
  454.8 0.6 maximum_bitcast_fusion
  (15 shorter events, 0.3 us)
Async XLA Ops:
  6.5 66.0 %copy-start.4 = (s32[3,1,1]{0,2,1:T(1,128)S(1)}, s32[3,1,1]{0,2,1:T(1,128)}, u32[]{:S(2)}) copy-start(s32[3,1,1]{0,2,1:T(1,128)} %param.21) | copy-start | bytes 40
  6.5 66.6 %copy-start.5 = (s32[3,1,1,8]{3,2,1,0:T(1,128)S(1)}, s32[3,1,1,8]{3,2,1,0:T(1,128)}, u32[]{:S(2)}) copy-start(s32[3,1,1,8]{3,2,1,0:T(1,128)} %param.20) | copy-start | bytes 292
  65.4 25.1 %all-to-all-start = ((bf16[8,8,16,256]{3,2,0,1:T(8,128)(2,1)}), bf16[8,8,16,256]{3,2,0,1:T(8,128)(2,1)S(1)}, u32[]{:S(2)}, u32[]{:S(2)}) async-start(bf16[8,8,16,256]{3,2,0,1:T(8,128)(2,1)} %copy.11), calls=%async_computation | async-start | bytes 1048576 | tf_op jit(solution)/shard_map/all_to_all | solution.py:67
  72.5 91.5 %reduce-scatter.4.cloned.1.call-start = ((), (), s32[]{:S(2)}) async-start(), calls=%async_computation.6 | async-start | bytes 147456 | tf_op jit(solution)/shard_map/reduce_scatter | solution.py:53
  90.7 22.0 %copy-start.3 = (f32[4,1,128,256]{3,2,1,0:T(8,128)S(1)}, f32[4,1,128,256]{3,2,1,0:T(8,128)}, u32[]{:S(2)}) copy-start(f32[4,1,128,256]{3,2,1,0:T(8,128)} %param.17) | copy-start | bytes 1572868
  112.0 0.7 copy-start.1
  216.7 22.7 %copy-start.7 = (s32[8]{0:T(128)S(1)}, s32[8]{0:T(128)}, u32[]{:S(2)}) copy-start(s32[8]{0:T(128)} %get-tuple-element.596) | copy-start | bytes 100
  216.7 22.6 %all-to-all-start.1 = ((bf16[8,8,16,256]{3,2,0,1:T(8,128)(2,1)}), bf16[8,8,16,256]{3,2,0,1:T(8,128)(2,1)S(1)}, u32[]{:S(2)}, u32[]{:S(2)}) async-start(bf16[8,8,16,256]{3,2,0,1:T(8,128)(2,1)} %copy.13), calls=%async_computation.2 | async-start | bytes 1048576 | tf_op jit(solution)/shard_map/all_to_all | solution.py:67
  221.3 91.8 %reduce-scatter.6.cloned.1.call-start = ((), (), s32[]{:S(2)}) async-start(), calls=%async_computation.7 | async-start | bytes 147456 | tf_op jit(solution)/shard_map/reduce_scatter | solution.py:53
  255.1 0.6 copy-start.2
  365.8 22.8 %copy-start.6 = (s32[8]{0:T(128)S(1)}, s32[8]{0:T(128)}, u32[]{:S(2)}) copy-start(s32[8]{0:T(128)} %get-tuple-element.644) | copy-start | bytes 100
  365.8 22.6 %all-to-all-start.2 = ((bf16[8,8,16,256]{3,2,0,1:T(8,128)(2,1)}), bf16[8,8,16,256]{3,2,0,1:T(8,128)(2,1)S(1)}, u32[]{:S(2)}, u32[]{:S(2)}) async-start(bf16[8,8,16,256]{3,2,0,1:T(8,128)(2,1)} %copy.15), calls=%async_computation.4 | async-start | bytes 1048576 | tf_op jit(solution)/shard_map/all_to_all | solution.py:67
  370.4 83.3 %reduce-scatter.8.cloned.1.call-start = ((), (), s32[]{:S(2)}) async-start(), calls=%async_computation.8 | async-start | bytes 147456 | tf_op jit(solution)/shard_map/reduce_scatter | solution.py:53
  401.1 0.6 copy-start
Sparse Core Ops, SparseCore 0:
  112.8 51.1 reduce-scatter.3
  255.9 57.1 reduce-scatter.5
  401.9 51.7 reduce-scatter.7
where the time goes:
time: 464 us; the launch traced here: 462 us
  waiting for transfers between devices  210 us (45%)
  blocking collectives  158 us (34%)
  loops' own time  34.9 us (8%)
  local copies, waits for them, and re-layouts  16.9 us (4%)
  starting transfers between devices  16.4 us (4%)
  between operations  13.3 us (3%)
  matrix products  12.3 us (3%)
    reduce_scatter x3, waiting for transfers between devices, shards(): lax.psum_scatter(partials[level_index], 'cols', scatter_dimension=0, tile...  161 us
    all_gather x3, blocking collectives, shards(): lax.all_gather(own_solution.astype(jnp.bfloat16)[None], 'rows', axis=0, t...  158 us
    all_to_all x3, waiting for transfers between devices, shards(): lax.all_to_all(grouped, 'cols', split_axis=1, concat_axis=2, tiled=True)  49.2 us
    another operation x3, loops' own time, slot_sum(): return lax.fori_loop(0, live_count, add_block, running)  34.9 us
    all_to_all x3, starting transfers between devices, shards(): lax.all_to_all(grouped, 'cols', split_axis=1, concat_axis=2, tiled=True)  16.3 us
  transfers between devices with their start and end apart: 6, of which 6 were waited for; matrix products, arithmetic and copies ran while one was open for 1% of the time, Pallas kernels for 0%

commit v1 on v0

--- a/solution.py
+++ b/solution.py
@@ -64,7 +64,19 @@
                 own_solution.astype(jnp.bfloat16)[None], "rows", axis=0, tiled=True
             )
             grouped = pieces.reshape(per_level, col_count, share_rows, block_width)
-            regrouped = lax.all_to_all(grouped, "cols", split_axis=1, concat_axis=2, tiled=True)
+            ways, here = (lax.axis_size("cols"), lax.axis_index("cols"))
+            width = grouped.shape[1] // ways
+            lengths = list(grouped.shape)
+            lengths[1] = width
+            height = lengths[2]
+            lengths[2] = height * ways
+            full = jnp.zeros(lengths, grouped.dtype)
+            for mask in range(ways):
+                part = lax.dynamic_slice_in_dim(grouped, (here ^ mask) * width, width, axis=1)
+                if mask:
+                    part = lax.ppermute(part, "cols", [(d, d ^ mask) for d in range(ways)])
+                full = lax.dynamic_update_slice_in_dim(full, part, (here ^ mask) * height, axis=2)
+            regrouped = full
             solved_store = solved_store.at[
                 level_index * per_level : (level_index + 1) * per_level
             ].set(regrouped[:, 0])

time: 464 us -> 508 us (1.095)
  starting transfers between devices: 16.4 us -> 81.1 us
  waiting for transfers between devices: 210 us -> 186 us
    ppermute x0 -> x21, starting transfers between devices: none -> 81 us  [shards(): part = lax.ppermute(part, 'cols', [(d, d ^ mask) for d in range(ways)])]
    all_to_all x3 -> x0, waiting for transfers between devices: 49.2 us -> none  [shards(): lax.all_to_all(grouped, 'cols', split_axis=1, concat_axis=2, tiled=True)]
    all_to_all x3 -> x0, starting transfers between devices: 16.3 us -> none  [shards(): lax.all_to_all(grouped, 'cols', split_axis=1, concat_axis=2, tiled=True)]
    ppermute x0 -> x21, waiting for transfers between devices: none -> 13.8 us  [shards(): part = lax.ppermute(part, 'cols', [(d, d ^ mask) for d in range(ways)])]
    reduce_scatter x3, waiting for transfers between devices: 161 us -> 172 us  [shards(): lax.psum_scatter(partials[level_index], 'cols', scatter_dimension=0, tile...]
    dynamic_slice x10, local copies, waits for them, and re-layouts: 6.43 us -> 11.9 us  [add_block(): source = chosen_ids[slot_index]]
  transfers between devices with their start and end apart: 6 -> 24, of which waited for: 6 -> 7; matrix products, arithmetic and copies ran while one was open for 1% -> 1% of each run, Pallas kernels for 0% -> 0%
where the time goes in v1:
time: 508 us; the launch traced here: 505 us
  waiting for transfers between devices  186 us (37%)
  blocking collectives  158 us (31%)
  starting transfers between devices  81.1 us (16%)
  loops' own time  31.9 us (6%)
  local copies, waits for them, and re-layouts  21.2 us (4%)
  between operations  13.8 us (3%)
  matrix products  12.9 us (3%)
    reduce_scatter x3, waiting for transfers between devices, shards(): lax.psum_scatter(partials[level_index], 'cols', scatter_dimension=0, tile...  172 us
    all_gather x3, blocking collectives, shards(): lax.all_gather(own_solution.astype(jnp.bfloat16)[None], 'rows', axis=0, t...  158 us
    ppermute x21, starting transfers between devices, shards(): part = lax.ppermute(part, 'cols', [(d, d ^ mask) for d in range(ways)])  81 us
    another operation x3, loops' own time, slot_sum(): return lax.fori_loop(0, live_count, add_block, running)  31.9 us
    ppermute x21, waiting for transfers between devices, shards(): part = lax.ppermute(part, 'cols', [(d, d ^ mask) for d in range(ways)])  13.8 us
    dynamic_slice x10, local copies, waits for them, and re-layouts, add_block(): source = chosen_ids[slot_index]  11.9 us
  transfers between devices with their start and end apart: 24, of which 7 were waited for; matrix products, arithmetic and copies ran while one was open for 1% of the time, Pallas kernels for 0%

profile of v1, /device:TPU:2, one launch (start us, length us, event | category | flops | bytes accessed | tf_op | source)
XLA Modules:
  0.0 505.3 jit_solution(14049875680792820309)
XLA Ops:
  6.5 0.9 slice.116
  7.5 1.0 fusion.36
  8.5 56.0 %all-gather = bf16[1024,256]{1,0:T(8,128)(2,1)S(1)} all-gather(bf16[16,256]{1,0:T(8,128)(2,1)S(1)} %get-tuple-element.446), channel_id=2, replica_groups=mesh['rows'=64,'cols'=8] {'rows'}, dimensions={0}, use_global_device_ids=true | all-gather | bytes 532480 | tf_op jit(solution)/shard_map/all_gather | solution.py:63
  64.5 3.5 collective-permute-start
  68.0 4.5 collective-permute-start.1
  72.5 2.1 collective-permute-start.2
  74.7 7.7 %collective-permute-start.3 = (bf16[8,1,16,256]{3,2,0,1:T(8,128)(2,1)S(1)}, bf16[8,1,16,256]{3,2,0,1:T(8,128)(2,1)S(1)}, u32[]{:S(2)}, u32[]{:S(2)}) collective-permute-start(bf16[8,1,16,256]{3,2,0,1:T(8,128)(2,1)S(1)} %get-tuple-element.436), channel_id=1, source_target_pairs={{0,4},{1,5},{2,6},{3,7},{4,0},{5,1},{6,2},{7,3},{8,12},{9,13},{10,... | collective-permute-start | bytes 196616 | tf_op jit(solution)/shard_map/ppermute | solution.py:77
  82.4 1.9 collective-permute-start.4
  84.4 3.5 slice_bitcast_fusion
  88.0 0.5 slice_bitcast_fusion.4
  88.6 0.6 fusion.35
  89.2 5.5 %collective-permute-start.5 = (bf16[8,1,16,256]{3,2,0,1:T(8,128)(2,1)S(1)}, bf16[8,1,16,256]{3,2,0,1:T(8,128)(2,1)S(1)}, u32[]{:S(2)}, u32[]{:S(2)}) collective-permute-start(bf16[8,1,16,256]{3,2,0,1:T(8,128)(2,1)S(1)} %get-tuple-element.434), channel_id=1, source_target_pairs={{0,6},{1,7},{2,4},{3,5},{4,2},{5,3},{6,0},{7,1},{8,14},{9,15},{10,... | collective-permute-start | bytes 196616 | tf_op jit(solution)/shard_map/ppermute | solution.py:77
  94.7 1.9 collective-permute-start.6
  96.8 1.7 collective-permute-done.5
  98.5 3.6 collective-permute-done.6
  102.3 21.6 %while.42 = (s32[]{:T(128)}, f32[128,256]{1,0:T(8,128)S(1)}, s32[]{:T(128)}, s32[8]{0:T(128)}, bf16[24,128,256]{2,1,0:T(8,128)(2,1)S(1)}, /*index=5*/bf16[8,256,...) while((s32[]{:T(128)}, f32[128,256]{1,0:T(8,128)S(1)}, ...), condition=%wide.region_1.2_spmd, body=%wide.region_0.0_spmd.sunk | while | flops 16810028 | bytes 459350 | solution.py:23
  103.0 1.2 dynamic_slice.261
  106.5 1.1 convolution_add_fusion.6
  108.2 1.2 dynamic_slice.261
  111.7 1.1 convolution_add_fusion.6
  113.5 1.2 dynamic_slice.261
  116.9 1.1 convolution_add_fusion.6
  118.7 1.2 dynamic_slice.261
  122.2 1.1 convolution_add_fusion.6
  123.9 0.6 copy-done.1
  124.6 1.1 fusion.34
  125.7 53.5 %reduce-scatter.4.cloned.1.call-done = f32[16,256]{1,0:T(8,128)} async-done(((f32[128,256]{1,0:T(8,128)}), f32[16,256]{1,0:T(8,128)}) %reduce-scatter.4.cloned.1.call-update) | async-done | bytes 16400 | tf_op jit(solution)/shard_map/reduce_scatter | solution.py:53
  179.2 1.5 fusion.37
  180.7 50.9 %all-gather.1 = bf16[1024,256]{1,0:T(8,128)(2,1)S(1)} all-gather(bf16[16,256]{1,0:T(8,128)(2,1)S(1)} %get-tuple-element.448), channel_id=3, replica_groups=mesh['rows'=64,'cols'=8] {'rows'}, dimensions={0}, use_global_device_ids=true | all-gather | bytes 532480 | tf_op jit(solution)/shard_map/all_gather | solution.py:63
  231.6 3.0 collective-permute-start.7
  234.6 4.6 collective-permute-start.8
  239.2 2.5 collective-permute-start.9
  241.7 5.2 %collective-permute-start.10 = (bf16[8,1,16,256]{3,2,0,1:T(8,128)(2,1)S(1)}, bf16[8,1,16,256]{3,2,0,1:T(8,128)(2,1)S(1)}, u32[]{:S(2)}, u32[]{:S(2)}) collective-permute-start(bf16[8,1,16,256]{3,2,0,1:T(8,128)(2,1)S(1)} %get-tuple-element.429), channel_id=1, source_target_pairs={{0,4},{1,5},{2,6},{3,7},{4,0},{5,1},{6,2},{7,3},{8,12},{9,13},{10,... | collective-permute-start | bytes 196616 | tf_op jit(solution)/shard_map/ppermute | solution.py:77
  246.9 3.3 collective-permute-start.11
  250.3 4.6 collective-permute-start.12
  255.0 3.7 collective-permute-start.13
  258.8 4.2 collective-permute-done.13
  263.1 15.7 %while.43 = (s32[]{:T(128)}, f32[128,256]{1,0:T(8,128)S(1)}, s32[]{:T(128)}, s32[8]{0:T(128)}, bf16[24,128,256]{2,1,0:T(8,128)(2,1)S(1)}, /*index=5*/bf16[8,256,...) while((s32[]{:T(128)}, f32[128,256]{1,0:T(8,128)S(1)}, ...), condition=%wide.region_4.5_spmd, body=%wide.region_3.4_spmd.sunk | while | flops 16810028 | bytes 459350 | solution.py:23
  263.7 1.2 dynamic_slice.264
  267.1 1.1 convolution_add_fusion.7
  268.7 1.2 dynamic_slice.264
  272.1 1.1 convolution_add_fusion.7
  273.8 1.2 dynamic_slice.264
  277.2 1.1 convolution_add_fusion.7
  278.8 0.6 copy-done.2
  279.5 60.2 %reduce-scatter.6.cloned.1.call-done = f32[16,256]{1,0:T(8,128)} async-done(((f32[128,256]{1,0:T(8,128)}), f32[16,256]{1,0:T(8,128)}) %reduce-scatter.6.cloned.1.call-update) | async-done | bytes 16400 | tf_op jit(solution)/shard_map/reduce_scatter | solution.py:53
  339.7 1.5 fusion.38
  341.2 50.9 %all-gather.2 = bf16[1024,256]{1,0:T(8,128)(2,1)S(1)} all-gather(bf16[16,256]{1,0:T(8,128)(2,1)S(1)} %get-tuple-element.450), channel_id=4, replica_groups=mesh['rows'=64,'cols'=8] {'rows'}, dimensions={0}, use_global_device_ids=true | all-gather | bytes 532480 | tf_op jit(solution)/shard_map/all_gather | solution.py:63
  392.2 3.0 collective-permute-start.14
  395.2 4.6 collective-permute-start.15
  399.8 2.5 collective-permute-start.16
  402.3 5.2 %collective-permute-start.17 = (bf16[8,1,16,256]{3,2,0,1:T(8,128)(2,1)S(1)}, bf16[8,1,16,256]{3,2,0,1:T(8,128)(2,1)S(1)}, u32[]{:S(2)}, u32[]{:S(2)}) collective-permute-start(bf16[8,1,16,256]{3,2,0,1:T(8,128)(2,1)S(1)} %get-tuple-element.422), channel_id=1, source_target_pairs={{0,4},{1,5},{2,6},{3,7},{4,0},{5,1},{6,2},{7,3},{8,12},{9,13},{10,... | collective-permute-start | bytes 196616 | tf_op jit(solution)/shard_map/ppermute | solution.py:77
  407.5 3.3 collective-permute-start.18
  410.9 4.6 collective-permute-start.19
  415.6 3.7 collective-permute-start.20
  419.4 4.2 collective-permute-done.20
  423.7 14.6 %while.44 = (s32[]{:T(128)}, f32[128,256]{1,0:T(8,128)S(1)}, s32[]{:T(128)}, s32[8]{0:T(128)}, bf16[24,128,256]{2,1,0:T(8,128)(2,1)S(1)}, /*index=5*/bf16[8,256,...) while((s32[]{:T(128)}, f32[128,256]{1,0:T(8,128)S(1)}, ...), condition=%wide.region_7.8_spmd, body=%wide.region_6.7_spmd.sunk | while | flops 16810028 | bytes 459350 | solution.py:23
  424.4 1.2 dynamic_slice.267
  429.0 1.2 dynamic_slice.267
  433.7 1.2 dynamic_slice.267
  438.3 0.6 copy-done
  439.0 58.2 %reduce-scatter.8.cloned.1.call-done = f32[16,256]{1,0:T(8,128)} async-done(((f32[128,256]{1,0:T(8,128)}), f32[16,256]{1,0:T(8,128)}) %reduce-scatter.8.cloned.1.call-update) | async-done | bytes 16400 | tf_op jit(solution)/shard_map/reduce_scatter | solution.py:53
  497.2 0.9 convolution_bitcast_fusion
  498.1 0.6 maximum_bitcast_fusion
  (75 shorter events, 1.5 us)
Async XLA Ops:
  6.5 172.7 %reduce-scatter.4.cloned.1.call-start = ((), (), s32[]{:S(2)}) async-start(), calls=%async_computation.3 | async-start | bytes 147456 | tf_op jit(solution)/shard_map/reduce_scatter | solution.py:53
  64.5 24.7 %collective-permute-start = (bf16[8,1,16,256]{3,2,0,1:T(8,128)(2,1)S(1)}, bf16[8,1,16,256]{3,2,0,1:T(8,128)(2,1)S(1)}, u32[]{:S(2)}, u32[]{:S(2)}) collective-permute-start(bf16[8,1,16,256]{3,2,0,1:T(8,128)(2,1)S(1)} %get-tuple-element.439), channel_id=1, source_target_pairs={{0,1},{1,0},{2,3},{3,2},{4,5},{5,4},{6,7},{7,6},{8,9},{9,8},{10,11... | collective-permute-start | bytes 196616 | tf_op jit(solution)/shard_map/ppermute | solution.py:77
  68.0 26.7 %collective-permute-start.1 = (bf16[8,1,16,256]{3,2,0,1:T(8,128)(2,1)S(1)}, bf16[8,1,16,256]{3,2,0,1:T(8,128)(2,1)S(1)}, u32[]{:S(2)}, u32[]{:S(2)}) collective-permute-start(bf16[8,1,16,256]{3,2,0,1:T(8,128)(2,1)S(1)} %get-tuple-element.438), channel_id=1, source_target_pairs={{0,2},{1,3},{2,0},{3,1},{4,6},{5,7},{6,4},{7,5},{8,10},{9,11},{10,... | collective-permute-start | bytes 196616 | tf_op jit(solution)/shard_map/ppermute | solution.py:77
  72.5 24.1 %collective-permute-start.2 = (bf16[8,1,16,256]{3,2,0,1:T(8,128)(2,1)S(1)}, bf16[8,1,16,256]{3,2,0,1:T(8,128)(2,1)S(1)}, u32[]{:S(2)}, u32[]{:S(2)}) collective-permute-start(bf16[8,1,16,256]{3,2,0,1:T(8,128)(2,1)S(1)} %get-tuple-element.437), channel_id=1, source_target_pairs={{0,3},{1,2},{2,1},{3,0},{4,7},{5,6},{6,5},{7,4},{8,11},{9,10},{10,... | collective-permute-start | bytes 196616 | tf_op jit(solution)/shard_map/ppermute | solution.py:77
  74.7 22.0 %collective-permute-start.3 = (bf16[8,1,16,256]{3,2,0,1:T(8,128)(2,1)S(1)}, bf16[8,1,16,256]{3,2,0,1:T(8,128)(2,1)S(1)}, u32[]{:S(2)}, u32[]{:S(2)}) collective-permute-start(bf16[8,1,16,256]{3,2,0,1:T(8,128)(2,1)S(1)} %get-tuple-element.436), channel_id=1, source_target_pairs={{0,4},{1,5},{2,6},{3,7},{4,0},{5,1},{6,2},{7,3},{8,12},{9,13},{10,... | collective-permute-start | bytes 196616 | tf_op jit(solution)/shard_map/ppermute | solution.py:77
  82.4 14.3 %collective-permute-start.4 = (bf16[8,1,16,256]{3,2,0,1:T(8,128)(2,1)S(1)}, bf16[8,1,16,256]{3,2,0,1:T(8,128)(2,1)S(1)}, u32[]{:S(2)}, u32[]{:S(2)}) collective-permute-start(bf16[8,1,16,256]{3,2,0,1:T(8,128)(2,1)S(1)} %get-tuple-element.435), channel_id=1, source_target_pairs={{0,5},{1,4},{2,7},{3,6},{4,1},{5,0},{6,3},{7,2},{8,13},{9,12},{10,... | collective-permute-start | bytes 196616 | tf_op jit(solution)/shard_map/ppermute | solution.py:77
  84.4 3.6 copy-start.7
  84.4 4.2 copy-start.6
  89.2 9.3 %collective-permute-start.5 = (bf16[8,1,16,256]{3,2,0,1:T(8,128)(2,1)S(1)}, bf16[8,1,16,256]{3,2,0,1:T(8,128)(2,1)S(1)}, u32[]{:S(2)}, u32[]{:S(2)}) collective-permute-start(bf16[8,1,16,256]{3,2,0,1:T(8,128)(2,1)S(1)} %get-tuple-element.434), channel_id=1, source_target_pairs={{0,6},{1,7},{2,4},{3,5},{4,2},{5,3},{6,0},{7,1},{8,14},{9,15},{10,... | collective-permute-start | bytes 196616 | tf_op jit(solution)/shard_map/ppermute | solution.py:77
  94.7 7.4 %collective-permute-start.6 = (bf16[8,1,16,256]{3,2,0,1:T(8,128)(2,1)S(1)}, bf16[8,1,16,256]{3,2,0,1:T(8,128)(2,1)S(1)}, u32[]{:S(2)}, u32[]{:S(2)}) collective-permute-start(bf16[8,1,16,256]{3,2,0,1:T(8,128)(2,1)S(1)} %get-tuple-element.433), channel_id=1, source_target_pairs={{0,7},{1,6},{2,5},{3,4},{4,3},{5,2},{6,1},{7,0},{8,15},{9,14},{10,... | collective-permute-start | bytes 196616 | tf_op jit(solution)/shard_map/ppermute | solution.py:77
  102.3 77.0 %copy-start.3 = (bf16[4,1,256,256]{3,2,1,0:T(8,128)(2,1)S(1)}, bf16[4,1,256,256]{3,2,1,0:T(8,128)(2,1)}, u32[]{:S(2)}) copy-start(bf16[4,1,256,256]{3,2,1,0:T(8,128)(2,1)} %param.19) | copy-start | bytes 1572868
  123.9 0.7 copy-start.1
  124.6 215.2 %reduce-scatter.6.cloned.1.call-start = ((), (), s32[]{:S(2)}) async-start(), calls=%async_computation.4 | async-start | bytes 147456 | tf_op jit(solution)/shard_map/reduce_scatter | solution.py:53
  231.6 18.7 %collective-permute-start.7 = (bf16[8,1,16,256]{3,2,0,1:T(8,128)(2,1)S(1)}, bf16[8,1,16,256]{3,2,0,1:T(8,128)(2,1)S(1)}, u32[]{:S(2)}, u32[]{:S(2)}) collective-permute-start(bf16[8,1,16,256]{3,2,0,1:T(8,128)(2,1)S(1)} %get-tuple-element.432), channel_id=1, source_target_pairs={{0,1},{1,0},{2,3},{3,2},{4,5},{5,4},{6,7},{7,6},{8,9},{9,8},{10,11... | collective-permute-start | bytes 196616 | tf_op jit(solution)/shard_map/ppermute | solution.py:77
  234.6 20.3 %collective-permute-start.8 = (bf16[8,1,16,256]{3,2,0,1:T(8,128)(2,1)S(1)}, bf16[8,1,16,256]{3,2,0,1:T(8,128)(2,1)S(1)}, u32[]{:S(2)}, u32[]{:S(2)}) collective-permute-start(bf16[8,1,16,256]{3,2,0,1:T(8,128)(2,1)S(1)} %get-tuple-element.431), channel_id=1, source_target_pairs={{0,2},{1,3},{2,0},{3,1},{4,6},{5,7},{6,4},{7,5},{8,10},{9,11},{10,... | collective-permute-start | bytes 196616 | tf_op jit(solution)/shard_map/ppermute | solution.py:77
  239.2 19.5 %collective-permute-start.9 = (bf16[8,1,16,256]{3,2,0,1:T(8,128)(2,1)S(1)}, bf16[8,1,16,256]{3,2,0,1:T(8,128)(2,1)S(1)}, u32[]{:S(2)}, u32[]{:S(2)}) collective-permute-start(bf16[8,1,16,256]{3,2,0,1:T(8,128)(2,1)S(1)} %get-tuple-element.430), channel_id=1, source_target_pairs={{0,3},{1,2},{2,1},{3,0},{4,7},{5,6},{6,5},{7,4},{8,11},{9,10},{10,... | collective-permute-start | bytes 196616 | tf_op jit(solution)/shard_map/ppermute | solution.py:77
  241.7 17.0 %collective-permute-start.10 = (bf16[8,1,16,256]{3,2,0,1:T(8,128)(2,1)S(1)}, bf16[8,1,16,256]{3,2,0,1:T(8,128)(2,1)S(1)}, u32[]{:S(2)}, u32[]{:S(2)}) collective-permute-start(bf16[8,1,16,256]{3,2,0,1:T(8,128)(2,1)S(1)} %get-tuple-element.429), channel_id=1, source_target_pairs={{0,4},{1,5},{2,6},{3,7},{4,0},{5,1},{6,2},{7,3},{8,12},{9,13},{10,... | collective-permute-start | bytes 196616 | tf_op jit(solution)/shard_map/ppermute | solution.py:77
  246.9 11.9 %collective-permute-start.11 = (bf16[8,1,16,256]{3,2,0,1:T(8,128)(2,1)S(1)}, bf16[8,1,16,256]{3,2,0,1:T(8,128)(2,1)S(1)}, u32[]{:S(2)}, u32[]{:S(2)}) collective-permute-start(bf16[8,1,16,256]{3,2,0,1:T(8,128)(2,1)S(1)} %get-tuple-element.428), channel_id=1, source_target_pairs={{0,5},{1,4},{2,7},{3,6},{4,1},{5,0},{6,3},{7,2},{8,13},{9,12},{10,... | collective-permute-start | bytes 196616 | tf_op jit(solution)/shard_map/ppermute | solution.py:77
  250.3 8.5 %collective-permute-start.12 = (bf16[8,1,16,256]{3,2,0,1:T(8,128)(2,1)S(1)}, bf16[8,1,16,256]{3,2,0,1:T(8,128)(2,1)S(1)}, u32[]{:S(2)}, u32[]{:S(2)}) collective-permute-start(bf16[8,1,16,256]{3,2,0,1:T(8,128)(2,1)S(1)} %get-tuple-element.427), channel_id=1, source_target_pairs={{0,6},{1,7},{2,4},{3,5},{4,2},{5,3},{6,0},{7,1},{8,14},{9,15},{10,... | collective-permute-start | bytes 196616 | tf_op jit(solution)/shard_map/ppermute | solution.py:77
  255.0 8.1 %collective-permute-start.13 = (bf16[8,1,16,256]{3,2,0,1:T(8,128)(2,1)S(1)}, bf16[8,1,16,256]{3,2,0,1:T(8,128)(2,1)S(1)}, u32[]{:S(2)}, u32[]{:S(2)}) collective-permute-start(bf16[8,1,16,256]{3,2,0,1:T(8,128)(2,1)S(1)} %get-tuple-element.426), channel_id=1, source_target_pairs={{0,7},{1,6},{2,5},{3,4},{4,3},{5,2},{6,1},{7,0},{8,15},{9,14},{10,... | collective-permute-start | bytes 196616 | tf_op jit(solution)/shard_map/ppermute | solution.py:77
  278.8 0.6 copy-start.2
  279.5 217.7 %reduce-scatter.8.cloned.1.call-start = ((), (), s32[]{:S(2)}) async-start(), calls=%async_computation.5 | async-start | bytes 147456 | tf_op jit(solution)/shard_map/reduce_scatter | solution.py:53
  392.2 18.7 %collective-permute-start.14 = (bf16[8,1,16,256]{3,2,0,1:T(8,128)(2,1)S(1)}, bf16[8,1,16,256]{3,2,0,1:T(8,128)(2,1)S(1)}, u32[]{:S(2)}, u32[]{:S(2)}) collective-permute-start(bf16[8,1,16,256]{3,2,0,1:T(8,128)(2,1)S(1)} %get-tuple-element.425), channel_id=1, source_target_pairs={{0,1},{1,0},{2,3},{3,2},{4,5},{5,4},{6,7},{7,6},{8,9},{9,8},{10,11... | collective-permute-start | bytes 196616 | tf_op jit(solution)/shard_map/ppermute | solution.py:77
  395.2 20.3 %collective-permute-start.15 = (bf16[8,1,16,256]{3,2,0,1:T(8,128)(2,1)S(1)}, bf16[8,1,16,256]{3,2,0,1:T(8,128)(2,1)S(1)}, u32[]{:S(2)}, u32[]{:S(2)}) collective-permute-start(bf16[8,1,16,256]{3,2,0,1:T(8,128)(2,1)S(1)} %get-tuple-element.424), channel_id=1, source_target_pairs={{0,2},{1,3},{2,0},{3,1},{4,6},{5,7},{6,4},{7,5},{8,10},{9,11},{10,... | collective-permute-start | bytes 196616 | tf_op jit(solution)/shard_map/ppermute | solution.py:77
  399.8 19.5 %collective-permute-start.16 = (bf16[8,1,16,256]{3,2,0,1:T(8,128)(2,1)S(1)}, bf16[8,1,16,256]{3,2,0,1:T(8,128)(2,1)S(1)}, u32[]{:S(2)}, u32[]{:S(2)}) collective-permute-start(bf16[8,1,16,256]{3,2,0,1:T(8,128)(2,1)S(1)} %get-tuple-element.423), channel_id=1, source_target_pairs={{0,3},{1,2},{2,1},{3,0},{4,7},{5,6},{6,5},{7,4},{8,11},{9,10},{10,... | collective-permute-start | bytes 196616 | tf_op jit(solution)/shard_map/ppermute | solution.py:77
  402.3 17.0 %collective-permute-start.17 = (bf16[8,1,16,256]{3,2,0,1:T(8,128)(2,1)S(1)}, bf16[8,1,16,256]{3,2,0,1:T(8,128)(2,1)S(1)}, u32[]{:S(2)}, u32[]{:S(2)}) collective-permute-start(bf16[8,1,16,256]{3,2,0,1:T(8,128)(2,1)S(1)} %get-tuple-element.422), channel_id=1, source_target_pairs={{0,4},{1,5},{2,6},{3,7},{4,0},{5,1},{6,2},{7,3},{8,12},{9,13},{10,... | collective-permute-start | bytes 196616 | tf_op jit(solution)/shard_map/ppermute | solution.py:77
  407.5 11.8 %collective-permute-start.18 = (bf16[8,1,16,256]{3,2,0,1:T(8,128)(2,1)S(1)}, bf16[8,1,16,256]{3,2,0,1:T(8,128)(2,1)S(1)}, u32[]{:S(2)}, u32[]{:S(2)}) collective-permute-start(bf16[8,1,16,256]{3,2,0,1:T(8,128)(2,1)S(1)} %get-tuple-element.421), channel_id=1, source_target_pairs={{0,5},{1,4},{2,7},{3,6},{4,1},{5,0},{6,3},{7,2},{8,13},{9,12},{10,... | collective-permute-start | bytes 196616 | tf_op jit(solution)/shard_map/ppermute | solution.py:77
  410.9 8.5 %collective-permute-start.19 = (bf16[8,1,16,256]{3,2,0,1:T(8,128)(2,1)S(1)}, bf16[8,1,16,256]{3,2,0,1:T(8,128)(2,1)S(1)}, u32[]{:S(2)}, u32[]{:S(2)}) collective-permute-start(bf16[8,1,16,256]{3,2,0,1:T(8,128)(2,1)S(1)} %get-tuple-element.420), channel_id=1, source_target_pairs={{0,6},{1,7},{2,4},{3,5},{4,2},{5,3},{6,0},{7,1},{8,14},{9,15},{10,... | collective-permute-start | bytes 196616 | tf_op jit(solution)/shard_map/ppermute | solution.py:77
  415.6 8.1 %collective-permute-start.20 = (bf16[8,1,16,256]{3,2,0,1:T(8,128)(2,1)S(1)}, bf16[8,1,16,256]{3,2,0,1:T(8,128)(2,1)S(1)}, u32[]{:S(2)}, u32[]{:S(2)}) collective-permute-start(bf16[8,1,16,256]{3,2,0,1:T(8,128)(2,1)S(1)} %get-tuple-element.419), channel_id=1, source_target_pairs={{0,7},{1,6},{2,5},{3,4},{4,3},{5,2},{6,1},{7,0},{8,15},{9,14},{10,... | collective-permute-start | bytes 196616 | tf_op jit(solution)/shard_map/ppermute | solution.py:77
  423.7 74.4 %copy-start.4 = (f32[16,256]{1,0:T(8,128)S(1)}, f32[16,256]{1,0:T(8,128)}, u32[]{:S(2)}) copy-start(f32[16,256]{1,0:T(8,128)} %get-tuple-element.449) | copy-start | bytes 49156
  423.7 74.4 %copy-start.5 = (f32[16,256]{1,0:T(8,128)S(1)}, f32[16,256]{1,0:T(8,128)}, u32[]{:S(2)}) copy-start(f32[16,256]{1,0:T(8,128)} %get-tuple-element.451) | copy-start | bytes 49156
  438.3 0.6 copy-start
Sparse Core Ops, SparseCore 0:
  124.7 54.4 reduce-scatter.3
  279.6 60.0 reduce-scatter.5
  439.1 58.0 reduce-scatter.7
